TPU v7x, 256 devices: a whole 4x4x8 slice. The times are simulated.
256 devices in a mesh: dom: 32 (over z, x), rep: 8 (over y, core).
Axes of the slice: x: 4, y: 4, z: 8, core: 2. Of those that a mesh axis runs over, the one named last changes fastest.
Arguments:
- grad_out: bfloat16 [262144, 512], P(('dom', 'rep')), may hold values from -6 to 6
- features: bfloat16 [262144, 512], P(('dom', 'rep')), may hold values from -24 to 24
- weight: bfloat16 [512, 512], replicated, may hold values from -0.25 to 0.25
- edge_blocks: bfloat16 [32768, 128, 128], P(('dom', 'rep')), may hold values from -0.25 to 0.25
- block_index: int32 [32768, 2], P(('dom', 'rep')), may hold values from 0 to 63, as said below
- block_count: int32 [256], P(('dom', 'rep')), may hold values from 25 to 128, as said below
- node_perm: int32 [262144], P(('dom', 'rep')), may hold values from 0 to 262143, as said below
Outputs:
- grad_input: bfloat16 [262144, 512], P(('dom', 'rep'))
- weight_grad: float32 [512, 512], P('dom', 'rep')
Inputs may be any that keep to these rules, and one draw needn't show every extreme that they name: A node at input row i, held by device s = i // 1024, lands at node_perm[i] = t * 1024 + s * 4 + k with 0 <= k < 4; each device's rows cover every pair (t, k) exactly once, so every device passes exactly 4 rows to every device. `block_index`: first column below 64, second below 8; blocks may repeat. `block_count`: in each group of 8 devices along rep exactly one device has 128 live slots; the others have between 25 and 64.
All inputs are finite; a program needn't handle non-finite values.
Results may differ from a plain program's by a relative error of at most 0.005.
Values may be sent and summed in bfloat16 or wider, within the bound.
A program may use at most 64 MiB of HBM per device.

v0:
```python
import math
import jax
import jax.numpy as jnp
from jax import lax
from jax.sharding import PartitionSpec as P


def cut_along(x, dim, length):
    before, after = (x.shape[:dim], x.shape[dim + 1 :])
    return jnp.moveaxis(x.reshape(*before, length, -1, *after), dim, 0)


def in_order(parts, dim):
    parts = jnp.moveaxis(parts, 0, dim)
    shape = parts.shape
    return parts.reshape(*shape[:dim], shape[dim] * shape[dim + 1], *shape[dim + 2 :])


def one_exchange(x, axis, axes, splits, concats):
    sizes = [lax.axis_size(a) for a in axes]
    parts = cut_along(x, splits[0], sizes[0])
    parts = jnp.moveaxis(cut_along(parts, splits[1] + 1, sizes[1]), 0, 1)
    inside = parts.shape[2:]
    parts = parts.reshape(-1, *inside)
    parts = lax.all_to_all(parts, axis, split_axis=0, concat_axis=0, tiled=True)
    parts = in_order(parts.reshape(*sizes, *inside), concats[0] + 1)
    return in_order(parts, concats[1])


def sent_and_summed(x, axis, dim):
    parts = cut_along(x, dim, lax.axis_size(axis))
    arrived = lax.all_to_all(parts, axis, split_axis=0, concat_axis=0, tiled=True)
    return arrived.sum(axis=0)


def accumulate(running, block_values, index_values, live_count, stacked):
    group_len = 16
    turn_count = (live_count + group_len - 1) // group_len

    def add_group(turn_index, current):
        first_slot = turn_index * group_len
        block_part = lax.dynamic_slice_in_dim(block_values, first_slot, group_len, 0)
        index_part = lax.dynamic_slice_in_dim(index_values, first_slot, group_len, 0)
        alive_mask = first_slot + jnp.arange(group_len) < live_count
        source = jnp.take(stacked, index_part[:, 0], axis=0)
        products = jnp.einsum(
            "kij,kif->kjf", block_part, source, preferred_element_type=jnp.float32
        )
        targets = index_part[:, 1]
        onehot = jnp.where(
            alive_mask[:, None] & (targets[:, None] == jnp.arange(current.shape[0])[None, :]),
            1.0,
            0.0,
        ).astype(jnp.float32)
        return current + jnp.einsum(
            "kc,kjf->cjf",
            onehot,
            products,
            precision=lax.Precision.HIGHEST,
            preferred_element_type=jnp.float32,
        )

    return lax.fori_loop(0, turn_count, add_group, running)


def on_device(grad_out, features, weight, edge_blocks, block_index, block_count, node_perm):
    dom_count = lax.axis_size("dom")
    rep_count = lax.axis_size("rep")
    device_count = dom_count * rep_count
    row_count = grad_out.shape[0]
    feat_width = grad_out.shape[1]
    slot_rows = row_count // device_count
    block_side = edge_blocks.shape[1]
    col_blocks = row_count // block_side
    target_device = node_perm // row_count
    within_slot = node_perm % slot_rows
    target_slot = target_device * slot_rows + within_slot
    ordered = jnp.zeros_like(grad_out).at[target_slot].set(grad_out)
    ordered = ordered.reshape(dom_count, rep_count, slot_rows, feat_width)
    arrived = one_exchange(ordered, ("dom", "rep"), ("dom", "rep"), (0, 1), (0, 1))
    local_rows = arrived.reshape(row_count, feat_width)
    whole = lax.all_gather(local_rows, "rep", axis=0, tiled=True)
    stacked = whole.reshape(-1, block_side, feat_width)
    running = jnp.zeros((col_blocks, block_side, feat_width), jnp.float32)
    running = accumulate(running, edge_blocks, block_index, block_count[0], stacked)
    aggregated = running.reshape(row_count, feat_width).astype(jnp.bfloat16)
    grad_input = lax.dot_general(
        aggregated, weight, (((1,), (1,)), ((), ())), preferred_element_type=jnp.float32
    ).astype(jnp.bfloat16)
    scale_factor = 1.0 / math.sqrt(row_count * device_count)
    partial_rows = sent_and_summed(
        lax.dot_general(
            features, aggregated, (((0,), (0,)), ((), ())), preferred_element_type=jnp.float32
        )
        * scale_factor,
        "dom",
        0,
    )
    weight_grad = sent_and_summed(partial_rows, "rep", 1)
    return (grad_input, weight_grad)


def solution(mesh):
    in_specs = (
        P(("dom", "rep"), None),
        P(("dom", "rep"), None),
        P(),
        P(("dom", "rep"), None, None),
        P(("dom", "rep"), None),
        P(("dom", "rep")),
        P(("dom", "rep")),
    )
    out_specs = (P(("dom", "rep"), None), P("dom", "rep"))
    return jax.shard_map(
        on_device, mesh=mesh, in_specs=in_specs, out_specs=out_specs, check_vma=False
    )
```

profile of v0, /device:TPU:1, one launch (start us, length us, event | category | flops | bytes accessed | tf_op | source)
XLA Modules:
  0.0 271.4 jit_solution(8153901035986305665)
XLA Ops:
  7.2 0.8 compare_select_fusion.1
  8.0 5.8 %scatter_custom_fusion = bf16[1024,512]{1,0:T(8,128)(2,1)S(1)} fusion(s32[1024]{0:T(1024)S(1)} %compare_select_fusion.1, bf16[1024,512]{1,0:T(8,128)(2,1)} %param.9, bf16[]{:T(256)} %constant.78.clone.1), kind=kCustom, calls=%fused_computation.32 | custom fusion | bytes 1049088 | tf_op jit(solution)/shard_map/scatter | solution.py:78
  14.1 45.9 %all_to_all.15 = bf16[256,1,1,4,512]{4,3,2,1,0:T(4,128)(2,1)S(1)} all-to-all(bf16[256,1,1,4,512]{4,3,2,1,0:T(4,128)(2,1)S(1)} %bitcast.38), channel_id=1, replica_groups=mesh['dom'=32,'rep'=8] {'dom','rep'}, dimensions={0} | all-to-all | bytes 2097152 | tf_op jit(solution)/shard_map/all_to_all | solution.py:25
  60.0 1.1 reshape_reshape.3
  61.8 46.9 %all-gather.2.cloned.1.call-done = bf16[8192,512]{1,0:T(8,128)(2,1)} async-done(((bf16[1024,512]{1,0:T(8,128)(2,1)}), bf16[8192,512]{1,0:T(8,128)(2,1)}) %all-gather.2.cloned.1.call-update) | async-done | bytes 8388624 | tf_op jit(solution)/shard_map/all_gather | solution.py:82
  108.7 1.7 broadcast_in_dim.29
  110.3 51.8 %while.10 = (s32[]{:T(128)}, f32[8,128,512]{2,0,1:T(8,128)}, s32[]{:T(128)}, s32[]{:T(128)}, s32[128,2]{0,1:T(2,128)S(1)}, /*index=5*/bf16[128,128,128]{2,1,0:T(...) while((s32[]{:T(128)}, f32[8,128,512]{2,0,1:T(8,128)}, ...), condition=%wide.region_2.3_spmd, body=%wide.region_1.2_spmd.sunk | while | flops 370673216 | bytes 19403756 | solution.py:63
  110.4 4.1 %gather_fusion = bf16[16,128,512]{2,1,0:T(8,128)(2,1)S(1)} fusion(bf16[64,128,512]{2,1,0:T(8,128)(2,1)} %get-tuple-element.147, s32[1024]{0:T(1024)S(1)} %pad_clamp_fusion.2), kind=kCustom, calls=%fused_computation.clone.1 | custom fusion | bytes 4194368 | tf_op jit(solution)/shard_map/while/body/jit(_take)/gather | solution.py:45
  114.5 1.8 fusion.44
  117.0 6.3 %fusion.45 = f32[8,128,512]{2,0,1:T(8,128)} fusion(f32[8,128,512]{2,0,1:T(8,128)} %get-tuple-element.131, f32[16,128,512]{2,1,0:T(8,128)S(1)} %fusion.44, s32[16]{0:T(128)S(1)} %get-tuple-element.118, pred[16]{0:T(512)(128)(4,1)S(1)} %add_compare_fusion.2), kind=kOutput, calls=%fused_computation.7.clone.1 | convolution fusion | flops 101187968 | bytes 8388688 | tf_op jit(solution)/shard_map/while/body/kc,kjf->cjf/dot_general | solution.py:55
  123.4 4.1 %gather_fusion = bf16[16,128,512]{2,1,0:T(8,128)(2,1)S(1)} fusion(bf16[64,128,512]{2,1,0:T(8,128)(2,1)} %get-tuple-element.147, s32[1024]{0:T(1024)S(1)} %pad_clamp_fusion.2), kind=kCustom, calls=%fused_computation.clone.1 | custom fusion | bytes 4194368 | tf_op jit(solution)/shard_map/while/body/jit(_take)/gather | solution.py:45
  127.4 1.8 fusion.44
  129.9 6.3 %fusion.45 = f32[8,128,512]{2,0,1:T(8,128)} fusion(f32[8,128,512]{2,0,1:T(8,128)} %get-tuple-element.131, f32[16,128,512]{2,1,0:T(8,128)S(1)} %fusion.44, s32[16]{0:T(128)S(1)} %get-tuple-element.118, pred[16]{0:T(512)(128)(4,1)S(1)} %add_compare_fusion.2), kind=kOutput, calls=%fused_computation.7.clone.1 | convolution fusion | flops 101187968 | bytes 8388688 | tf_op jit(solution)/shard_map/while/body/kc,kjf->cjf/dot_general | solution.py:55
  136.3 4.1 %gather_fusion = bf16[16,128,512]{2,1,0:T(8,128)(2,1)S(1)} fusion(bf16[64,128,512]{2,1,0:T(8,128)(2,1)} %get-tuple-element.147, s32[1024]{0:T(1024)S(1)} %pad_clamp_fusion.2), kind=kCustom, calls=%fused_computation.clone.1 | custom fusion | bytes 4194368 | tf_op jit(solution)/shard_map/while/body/jit(_take)/gather | solution.py:45
  140.4 1.8 fusion.44
  142.9 6.3 %fusion.45 = f32[8,128,512]{2,0,1:T(8,128)} fusion(f32[8,128,512]{2,0,1:T(8,128)} %get-tuple-element.131, f32[16,128,512]{2,1,0:T(8,128)S(1)} %fusion.44, s32[16]{0:T(128)S(1)} %get-tuple-element.118, pred[16]{0:T(512)(128)(4,1)S(1)} %add_compare_fusion.2), kind=kOutput, calls=%fused_computation.7.clone.1 | convolution fusion | flops 101187968 | bytes 8388688 | tf_op jit(solution)/shard_map/while/body/kc,kjf->cjf/dot_general | solution.py:55
  149.2 4.1 %gather_fusion = bf16[16,128,512]{2,1,0:T(8,128)(2,1)S(1)} fusion(bf16[64,128,512]{2,1,0:T(8,128)(2,1)} %get-tuple-element.147, s32[1024]{0:T(1024)S(1)} %pad_clamp_fusion.2), kind=kCustom, calls=%fused_computation.clone.1 | custom fusion | bytes 4194368 | tf_op jit(solution)/shard_map/while/body/jit(_take)/gather | solution.py:45
  153.3 1.8 fusion.44
  155.8 6.3 %fusion.45 = f32[8,128,512]{2,0,1:T(8,128)} fusion(f32[8,128,512]{2,0,1:T(8,128)} %get-tuple-element.131, f32[16,128,512]{2,1,0:T(8,128)S(1)} %fusion.44, s32[16]{0:T(128)S(1)} %get-tuple-element.118, pred[16]{0:T(512)(128)(4,1)S(1)} %add_compare_fusion.2), kind=kOutput, calls=%fused_computation.7.clone.1 | convolution fusion | flops 101187968 | bytes 8388688 | tf_op jit(solution)/shard_map/while/body/kc,kjf->cjf/dot_general | solution.py:55
  162.1 2.7 copy.25
  165.6 85.4 %all_to_all.16 = f32[32,16,512]{2,1,0:T(8,128)S(1)} all-to-all(f32[32,16,512]{2,1,0:T(8,128)S(1)} %bitcast.42), channel_id=1, replica_groups=mesh['dom'=32,'rep'=8] {'dom'}, dimensions={0} | all-to-all | bytes 2097152 | tf_op jit(solution)/shard_map/all_to_all | solution.py:32
  251.9 6.0 %all-to-all-start.2 = ((f32[8,1,1024]{2,1,0:T(1,128)}), f32[8,1,1024]{2,1,0:T(1,128)S(1)}, u32[]{:S(2)}, u32[]{:S(2)}) async-start(f32[8,1,1024]{2,1,0:T(1,128)} %reshape.55), calls=%async_computation.2 | async-start | bytes 65536 | tf_op jit(solution)/shard_map/all_to_all | solution.py:32
  257.9 2.7 %convolution_convert_fusion = bf16[1024,512]{1,0:T(8,128)(2,1)} fusion(bf16[1024,512]{1,0:T(8,128)(2,1)S(1)} %bitcast.41, bf16[512,512]{1,0:T(8,128)(2,1)} %param.11), kind=kOutput, calls=%fused_computation.30 | convolution fusion | flops 537395200 | bytes 2621440 | tf_op jit(solution)/shard_map/dot_general | solution.py:87
  260.7 2.0 all-to-all-done.2
  (36 shorter events, 6.9 us)
Async XLA Ops:
  7.2 157.7 %copy-start = (bf16[1024,512]{1,0:T(8,128)(2,1)S(1)}, bf16[1024,512]{1,0:T(8,128)(2,1)}, u32[]{:S(2)}) copy-start(bf16[1024,512]{1,0:T(8,128)(2,1)} %param.10) | copy-start | bytes 3145732
  7.2 101.5 %all-gather.2.cloned.1.call-start = ((), (), s32[]{:S(2)}) async-start(), calls=%async_computation.3 | async-start | bytes 9437184 | tf_op jit(solution)/shard_map/all_gather | solution.py:82
  61.1 49.2 %copy-start.1 = (s32[128,2]{0,1:T(2,128)S(1)}, s32[128,2]{0,1:T(2,128)}, u32[]{:S(2)}) copy-start(s32[128,2]{0,1:T(2,128)} %param.13) | copy-start | bytes 3076
  251.9 10.8 %all-to-all-start.2 = ((f32[8,1,1024]{2,1,0:T(1,128)}), f32[8,1,1024]{2,1,0:T(1,128)S(1)}, u32[]{:S(2)}, u32[]{:S(2)}) async-start(f32[8,1,1024]{2,1,0:T(1,128)} %reshape.55), calls=%async_computation.2 | async-start | bytes 65536 | tf_op jit(solution)/shard_map/all_to_all | solution.py:32
Sparse Core Ops, SparseCore 0:
  61.2 47.3 all-gather.1
where the time goes:
time: 273 us; the launch traced here: 271 us
  blocking collectives  131 us (48%)
  waiting for transfers between devices  48.9 us (18%)
  matrix products  35.9 us (13%)
  local copies, waits for them, and re-layouts  29.5 us (11%)
  between operations  14.8 us (5%)
  starting transfers between devices  6.07 us (2%)
  other arithmetic  4.88 us (2%)
    all_to_all x1, blocking collectives, sent_and_summed(): lax.all_to_all(parts, axis, split_axis=0, concat_axis=0, tiled=True)  85.4 us
    all_gather x1, waiting for transfers between devices, on_device(): whole = lax.all_gather(local_rows, 'rep', axis=0, tiled=True)  46.9 us
    all_to_all x1, blocking collectives, one_exchange(): parts = lax.all_to_all(parts, axis, split_axis=0, concat_axis=0, tiled=True)  45.9 us
    dot_general x4, matrix products, add_group(): jnp.einsum('kc,kjf->cjf', onehot, products, precision=lax.Precision.HIGHE...  25.1 us
    gather x4, local copies, waits for them, and re-layouts, add_group(): source = jnp.take(stacked, index_part[:, 0], axis=0)  16.2 us
    dot_general x4, matrix products, add_group(): jnp.einsum('kij,kif->kjf', block_part, source, preferred_element_type=jnp...  7.32 us
    all_to_all x1, starting transfers between devices, sent_and_summed(): lax.all_to_all(parts, axis, split_axis=0, concat_axis=0, tiled=True)  6.03 us
    scatter x1, local copies, waits for them, and re-layouts, on_device(): ordered = jnp.zeros_like(grad_out).at[target_slot].set(grad_out)  5.84 us
  transfers between devices with their start and end apart: 2, of which 2 were waited for; matrix products, arithmetic and copies ran while one was open for 1% of the time, Pallas kernels for 0%

commit v1 on v0

--- a/solution.py
+++ b/solution.py
@@ -79,7 +79,9 @@
     ordered = ordered.reshape(dom_count, rep_count, slot_rows, feat_width)
     arrived = one_exchange(ordered, ("dom", "rep"), ("dom", "rep"), (0, 1), (0, 1))
     local_rows = arrived.reshape(row_count, feat_width)
-    whole = lax.all_gather(local_rows, "rep", axis=0, tiled=True)
+    whole = jnp.concatenate(
+        lax.all_to_all(jnp.stack([local_rows] * lax.axis_size("rep")), "rep", 0, 0), axis=0
+    )
     stacked = whole.reshape(-1, block_side, feat_width)
     running = jnp.zeros((col_blocks, block_side, feat_width), jnp.float32)
     running = accumulate(running, edge_blocks, block_index, block_count[0], stacked)

time: 273 us -> 312 us (1.14)
  waiting for transfers between devices: 48.9 us -> 95 us
  between operations: 14.8 us -> 1.39 us
  starting transfers between devices: 6.07 us -> 12.2 us
    all_to_all x0 -> x1, waiting for transfers between devices: none -> 93.1 us  [on_device(): lax.all_to_all(jnp.stack([local_rows] * lax.axis_size('rep')), 'rep', 0, 0)]
    all_gather x1 -> x0, waiting for transfers between devices: 46.9 us -> none  [on_device(): whole = lax.all_gather(local_rows, 'rep', axis=0, tiled=True)]
    all_to_all x0 -> x1, starting transfers between devices: none -> 6.33 us  [on_device(): lax.all_to_all(jnp.stack([local_rows] * lax.axis_size('rep')), 'rep', 0, 0)]
    all_to_all x1, blocking collectives: 85.4 us -> 82.1 us  [sent_and_summed(): lax.all_to_all(parts, axis, split_axis=0, concat_axis=0, tiled=True)]
where the time goes in v1:
time: 312 us; the launch traced here: 310 us
  blocking collectives  128 us (41%)
  waiting for transfers between devices  95 us (30%)
  matrix products  36 us (12%)
  local copies, waits for them, and re-layouts  32.6 us (10%)
  starting transfers between devices  12.2 us (4%)
  other arithmetic  4.89 us (2%)
    all_to_all x1, waiting for transfers between devices, on_device(): lax.all_to_all(jnp.stack([local_rows] * lax.axis_size('rep')), 'rep', 0, 0)  93.1 us
    all_to_all x1, blocking collectives, sent_and_summed(): lax.all_to_all(parts, axis, split_axis=0, concat_axis=0, tiled=True)  82.1 us
    all_to_all x1, blocking collectives, one_exchange(): parts = lax.all_to_all(parts, axis, split_axis=0, concat_axis=0, tiled=True)  45.9 us
    dot_general x4, matrix products, add_group(): jnp.einsum('kc,kjf->cjf', onehot, products, precision=lax.Precision.HIGHE...  25.1 us
    gather x4, local copies, waits for them, and re-layouts, add_group(): source = jnp.take(stacked, index_part[:, 0], axis=0)  16.2 us
    dot_general x4, matrix products, add_group(): jnp.einsum('kij,kif->kjf', block_part, source, preferred_element_type=jnp...  7.32 us
    all_to_all x1, starting transfers between devices, on_device(): lax.all_to_all(jnp.stack([local_rows] * lax.axis_size('rep')), 'rep', 0, 0)  6.33 us
  transfers between devices with their start and end apart: 2, of which 2 were waited for; matrix products, arithmetic and copies ran while one was open for 1% of the time, Pallas kernels for 0%

profile of v1, /device:TPU:1, one launch (start us, length us, event | category | flops | bytes accessed | tf_op | source)
XLA Modules:
  0.0 310.2 jit_solution(10368401668536445255)
XLA Ops:
  1.4 5.8 %scatter_custom_fusion = bf16[1024,512]{1,0:T(8,128)(2,1)S(1)} fusion(s32[1024]{0:T(1024)S(1)} %compare_select_fusion.1, bf16[1024,512]{1,0:T(8,128)(2,1)} %param.9, bf16[]{:T(256)} %constant.78.clone.1), kind=kCustom, calls=%fused_computation.32 | custom fusion | bytes 1049088 | tf_op jit(solution)/shard_map/scatter | solution.py:78
  7.6 45.9 %all_to_all.20 = bf16[256,1,1,4,512]{4,3,2,1,0:T(4,128)(2,1)S(1)} all-to-all(bf16[256,1,1,4,512]{4,3,2,1,0:T(4,128)(2,1)S(1)} %bitcast.37), channel_id=1, replica_groups=mesh['dom'=32,'rep'=8] {'dom','rep'}, dimensions={0} | all-to-all | bytes 2097152 | tf_op jit(solution)/shard_map/all_to_all | solution.py:25
  53.7 3.9 %stack.3 = bf16[8,1024,512]{2,1,0:T(8,128)(2,1)} broadcast(bf16[1024,512]{1,0:T(8,128)(2,1)S(1)} %stack_reshape_reshape.2), dimensions={1,2} | broadcast | bytes 9437184 | tf_op jit(solution)/shard_map/stack | solution.py:83
  57.6 6.3 %all-to-all-start.1 = ((bf16[8,1024,512]{2,1,0:T(8,128)(2,1)}), bf16[8,1024,512]{2,1,0:T(8,128)(2,1)}, u32[]{:S(2)}, u32[]{:S(2)}) async-start(bf16[8,1024,512]{2,1,0:T(8,128)(2,1)} %stack.3), calls=%async_computation.1 | async-start | bytes 16777216 | tf_op jit(solution)/shard_map/all_to_all | solution.py:83
  64.7 93.1 %all-to-all-done.1 = bf16[8,1024,512]{2,1,0:T(8,128)(2,1)} async-done(((bf16[8,1024,512]{2,1,0:T(8,128)(2,1)}), bf16[8,1024,512]{2,1,0:T(8,128)(2,1)}, u32[]{:S(2)}, u32[]{:S(2)}) %all-to-all-start.1) | async-done | bytes 8388640 | tf_op jit(solution)/shard_map/all_to_all | solution.py:83
  157.7 1.7 broadcast_in_dim.29
  159.4 51.8 %while.10 = (s32[]{:T(128)}, f32[8,128,512]{2,0,1:T(8,128)}, s32[]{:T(128)}, s32[]{:T(128)}, s32[128,2]{0,1:T(2,128)S(1)}, /*index=5*/bf16[128,128,128]{2,1,0:T(...) while((s32[]{:T(128)}, f32[8,128,512]{2,0,1:T(8,128)}, ...), condition=%wide.region_2.3_spmd, body=%wide.region_1.2_spmd.sunk | while | flops 370673216 | bytes 19403756 | solution.py:63
  159.5 4.1 %gather_fusion = bf16[16,128,512]{2,1,0:T(8,128)(2,1)S(1)} fusion(bf16[64,128,512]{2,1,0:T(8,128)(2,1)} %get-tuple-element.147, s32[1024]{0:T(1024)S(1)} %pad_clamp_fusion.2), kind=kCustom, calls=%fused_computation.clone.1 | custom fusion | bytes 4194368 | tf_op jit(solution)/shard_map/while/body/jit(_take)/gather | solution.py:45
  163.6 1.8 fusion.44
  166.1 6.3 %fusion.45 = f32[8,128,512]{2,0,1:T(8,128)} fusion(f32[8,128,512]{2,0,1:T(8,128)} %get-tuple-element.131, f32[16,128,512]{2,1,0:T(8,128)S(1)} %fusion.44, s32[16]{0:T(128)S(1)} %get-tuple-element.118, pred[16]{0:T(512)(128)(4,1)S(1)} %add_compare_fusion.2), kind=kOutput, calls=%fused_computation.7.clone.1 | convolution fusion | flops 101187968 | bytes 8388688 | tf_op jit(solution)/shard_map/while/body/kc,kjf->cjf/dot_general | solution.py:55
  172.4 4.1 %gather_fusion = bf16[16,128,512]{2,1,0:T(8,128)(2,1)S(1)} fusion(bf16[64,128,512]{2,1,0:T(8,128)(2,1)} %get-tuple-element.147, s32[1024]{0:T(1024)S(1)} %pad_clamp_fusion.2), kind=kCustom, calls=%fused_computation.clone.1 | custom fusion | bytes 4194368 | tf_op jit(solution)/shard_map/while/body/jit(_take)/gather | solution.py:45
  176.5 1.8 fusion.44
  179.0 6.3 %fusion.45 = f32[8,128,512]{2,0,1:T(8,128)} fusion(f32[8,128,512]{2,0,1:T(8,128)} %get-tuple-element.131, f32[16,128,512]{2,1,0:T(8,128)S(1)} %fusion.44, s32[16]{0:T(128)S(1)} %get-tuple-element.118, pred[16]{0:T(512)(128)(4,1)S(1)} %add_compare_fusion.2), kind=kOutput, calls=%fused_computation.7.clone.1 | convolution fusion | flops 101187968 | bytes 8388688 | tf_op jit(solution)/shard_map/while/body/kc,kjf->cjf/dot_general | solution.py:55
  185.4 4.1 %gather_fusion = bf16[16,128,512]{2,1,0:T(8,128)(2,1)S(1)} fusion(bf16[64,128,512]{2,1,0:T(8,128)(2,1)} %get-tuple-element.147, s32[1024]{0:T(1024)S(1)} %pad_clamp_fusion.2), kind=kCustom, calls=%fused_computation.clone.1 | custom fusion | bytes 4194368 | tf_op jit(solution)/shard_map/while/body/jit(_take)/gather | solution.py:45
  189.4 1.8 fusion.44
  191.9 6.3 %fusion.45 = f32[8,128,512]{2,0,1:T(8,128)} fusion(f32[8,128,512]{2,0,1:T(8,128)} %get-tuple-element.131, f32[16,128,512]{2,1,0:T(8,128)S(1)} %fusion.44, s32[16]{0:T(128)S(1)} %get-tuple-element.118, pred[16]{0:T(512)(128)(4,1)S(1)} %add_compare_fusion.2), kind=kOutput, calls=%fused_computation.7.clone.1 | convolution fusion | flops 101187968 | bytes 8388688 | tf_op jit(solution)/shard_map/while/body/kc,kjf->cjf/dot_general | solution.py:55
  198.3 4.1 %gather_fusion = bf16[16,128,512]{2,1,0:T(8,128)(2,1)S(1)} fusion(bf16[64,128,512]{2,1,0:T(8,128)(2,1)} %get-tuple-element.147, s32[1024]{0:T(1024)S(1)} %pad_clamp_fusion.2), kind=kCustom, calls=%fused_computation.clone.1 | custom fusion | bytes 4194368 | tf_op jit(solution)/shard_map/while/body/jit(_take)/gather | solution.py:45
  202.4 1.8 fusion.44
  204.9 6.3 %fusion.45 = f32[8,128,512]{2,0,1:T(8,128)} fusion(f32[8,128,512]{2,0,1:T(8,128)} %get-tuple-element.131, f32[16,128,512]{2,1,0:T(8,128)S(1)} %fusion.44, s32[16]{0:T(128)S(1)} %get-tuple-element.118, pred[16]{0:T(512)(128)(4,1)S(1)} %add_compare_fusion.2), kind=kOutput, calls=%fused_computation.7.clone.1 | convolution fusion | flops 101187968 | bytes 8388688 | tf_op jit(solution)/shard_map/while/body/kc,kjf->cjf/dot_general | solution.py:55
  211.2 2.7 copy.25
  214.7 82.1 %all_to_all.21 = f32[32,16,512]{2,1,0:T(8,128)S(1)} all-to-all(f32[32,16,512]{2,1,0:T(8,128)S(1)} %bitcast.41), channel_id=1, replica_groups=mesh['dom'=32,'rep'=8] {'dom'}, dimensions={0} | all-to-all | bytes 2097152 | tf_op jit(solution)/shard_map/all_to_all | solution.py:32
  297.7 5.9 %all-to-all-start.3 = ((f32[8,1,1024]{2,1,0:T(1,128)}), f32[8,1,1024]{2,1,0:T(1,128)S(1)}, u32[]{:S(2)}, u32[]{:S(2)}) async-start(f32[8,1,1024]{2,1,0:T(1,128)} %reshape.53), calls=%async_computation.3 | async-start | bytes 65536 | tf_op jit(solution)/shard_map/all_to_all | solution.py:32
  303.6 2.8 convolution_convert_fusion
  306.3 2.0 all-to-all-done.3
  (36 shorter events, 7.9 us)
Async XLA Ops:
  0.6 213.3 %copy-start = (bf16[1024,512]{1,0:T(8,128)(2,1)S(1)}, bf16[1024,512]{1,0:T(8,128)(2,1)}, u32[]{:S(2)}) copy-start(bf16[1024,512]{1,0:T(8,128)(2,1)} %param.10) | copy-start | bytes 3145732
  57.6 100.1 %all-to-all-start.1 = ((bf16[8,1024,512]{2,1,0:T(8,128)(2,1)}), bf16[8,1024,512]{2,1,0:T(8,128)(2,1)}, u32[]{:S(2)}, u32[]{:S(2)}) async-start(bf16[8,1024,512]{2,1,0:T(8,128)(2,1)} %stack.3), calls=%async_computation.1 | async-start | bytes 16777216 | tf_op jit(solution)/shard_map/all_to_all | solution.py:83
  64.0 95.4 %copy-start.1 = (s32[128,2]{0,1:T(2,128)S(1)}, s32[128,2]{0,1:T(2,128)}, u32[]{:S(2)}) copy-start(s32[128,2]{0,1:T(2,128)} %param.13) | copy-start | bytes 3076
  297.7 10.6 %all-to-all-start.3 = ((f32[8,1,1024]{2,1,0:T(1,128)}), f32[8,1,1024]{2,1,0:T(1,128)S(1)}, u32[]{:S(2)}, u32[]{:S(2)}) async-start(f32[8,1,1024]{2,1,0:T(1,128)} %reshape.53), calls=%async_computation.3 | async-start | bytes 65536 | tf_op jit(solution)/shard_map/all_to_all | solution.py:32
